TPU v7x, 256 devices: a whole 4x4x8 slice. The times are simulated.
256 devices in a mesh: dp: 4 (over y), fsdp: 8 (over z), tensor: 8 (over x, core).
Axes of the slice: x: 4, y: 4, z: 8, core: 2. Of those that a mesh axis runs over, the one named last changes fastest.
Arguments:
- momentum: bfloat16 [4, 8192, 8192], P('dp', 'fsdp', 'tensor'), may hold values from -24 to 24
- gradient: bfloat16 [4, 8192, 8192], P('dp', 'fsdp', 'tensor'), may hold values from -4 to 4
- factor: float32 [8192, 256], P('tensor'), may hold values from -6 to 6
Outputs:
- new_momentum: float32 [4, 8192, 8192], P('dp', 'fsdp', 'tensor')
- step_direction: bfloat16 [8192, 8192], P('fsdp', 'tensor')
- new_factor: float32 [8192, 256], P('tensor')
All inputs are finite; a program needn't handle non-finite values.
Results may differ from a plain program's by a relative error of at most 0.0065.
Values may be sent and summed in bfloat16 or wider, within the bound.
A program may use at most 64 MiB of HBM per device.

v0:
```python
import jax
import jax.numpy as jnp
from jax import lax
from jax.sharding import PartitionSpec as P

ROWS = 8192
COLS = 8192
RANK = 256


def orthonormal(rows_part, gram):
    lower = jnp.linalg.cholesky(gram)
    return jax.scipy.linalg.solve_triangular(lower, rows_part.T, lower=True).T


def transposed_product(block, ortho_low):
    return lax.dot_general(
        block, ortho_low, (((0,), (0,)), ((), ())), preferred_element_type=jnp.float32
    )


def local(momentum, gradient, factor):
    highest = lax.Precision.HIGHEST
    replicas = lax.axis_size("dp")
    moment = momentum[0]
    change = gradient[0]
    factor_low = factor.astype(jnp.bfloat16)
    partial_left = jnp.dot(moment, factor_low, preferred_element_type=jnp.float32)
    partial_left = partial_left + jnp.dot(change, factor_low, preferred_element_type=jnp.float32)
    left = lax.psum(partial_left, ("dp", "tensor")) / replicas
    gram = lax.psum(jnp.dot(left.T, left, precision=highest), "fsdp")
    ortho_low = orthonormal(left, gram).astype(jnp.bfloat16)
    partial_right = transposed_product(moment, ortho_low) + transposed_product(change, ortho_low)
    right = lax.psum(partial_right, ("dp", "fsdp")) / replicas
    square_sums = lax.psum(jnp.sum(right * right, axis=0), "tensor")
    new_factor = right / jnp.sqrt(square_sums / COLS + 1e-06)
    right_low = right.astype(jnp.bfloat16)
    feedback = jnp.dot(ortho_low, right_low.T, preferred_element_type=jnp.float32)
    new_momentum = (moment.astype(jnp.float32) + change.astype(jnp.float32) - 0.05 * feedback)[None]
    step_scale = jnp.sqrt(jnp.float32(ROWS / RANK))
    factor_next_low = new_factor.astype(jnp.bfloat16)
    step_direction = (
        step_scale * jnp.dot(ortho_low, factor_next_low.T, preferred_element_type=jnp.float32)
    ).astype(jnp.bfloat16)
    return (new_momentum, step_direction, new_factor)


def solution(mesh):
    in_specs = (P("dp", "fsdp", "tensor"), P("dp", "fsdp", "tensor"), P("tensor", None))
    out_specs = (P("dp", "fsdp", "tensor"), P("fsdp", "tensor"), P("tensor", None))
    return jax.shard_map(local, mesh=mesh, in_specs=in_specs, out_specs=out_specs, check_vma=False)
```

profile of v0, /device:TPU:1, one launch (start us, length us, event | category | flops | bytes accessed | tf_op | source)
XLA Modules:
  0.0 455.1 jit_solution(12589717732364756060)
XLA Ops:
  7.2 0.0 copy-start.1
  7.2 0.0 all-reduce.5.cloned.1.call-start
  7.2 2.7 fusion.2
  10.0 0.0 copy-done.7
  10.0 0.1 copy-done.1
  10.0 1.7 fusion.8
  11.7 0.0 all-reduce.5.cloned.1.call-update
  11.7 0.0 all-reduce.7.cloned.1.call-start
  11.8 119.2 %all-reduce.5.cloned.1.call-done = f32[1024,256]{1,0:T(8,128)} async-done(((f32[1024,256]{1,0:T(8,128)}), f32[1024,256]{1,0:T(8,128)}) %all-reduce.5.cloned.1.call-update) | async-done | bytes 1048592 | tf_op jit(solution)/shard_map/psum | solution.py:30
  131.0 4.2 fusion.17
  135.2 0.0 all-reduce.7.cloned.1.call-update
  135.2 0.2 all-reduce.9.cloned.1.call-start
  135.5 0.1 multiply_bitcast_fusion
  135.5 67.4 %all-reduce.7.cloned.1.call-done = f32[256,256]{0,1:T(8,128)} async-done(((f32[256,256]{0,1:T(8,128)}), f32[256,256]{0,1:T(8,128)}) %all-reduce.7.cloned.1.call-update) | async-done | bytes 262160 | tf_op jit(solution)/shard_map/psum | solution.py:31
  203.0 1.1 copy.7
  204.1 1.0 fusion.24
  205.1 11.7 %cholesky.50 = f32[128,128]{1,0:T(8,128)S(1)} custom-call(f32[128,128]{1,0:T(8,128)S(1)} %cholesky.118), custom_call_target="Cholesky" | custom-call | tf_op jit(solution)/shard_map/jit(cholesky)/cholesky | solution.py:12
  216.8 9.8 %custom-call.15 = f32[1,128,128]{1,2,0:T(8,128)S(1)} custom-call(f32[1,128,128]{2,1,0:T(8,128)S(1)} %get-tuple-element.24), custom_call_target="InvertDiagBlocksLowerTriangular" | custom-call | tf_op jit(solution)/shard_map/jit(cholesky)/cholesky | solution.py:12
  226.7 0.2 constant_dynamic-update-slice_fusion.1
  226.9 0.3 convolution_subtract_fusion.1
  227.1 11.7 %cholesky.105 = f32[128,128]{1,0:T(8,128)S(1)} custom-call(f32[128,128]{1,0:T(8,128)S(1)} %convolution_subtract_fusion.1), custom_call_target="Cholesky" | custom-call | tf_op jit(solution)/shard_map/jit(cholesky)/cholesky | solution.py:12
  238.9 0.6 compare_reduce_fusion
  240.8 0.7 select_select_fusion
  241.6 0.1 triangular_solve.57
  241.6 5.8 %while.1 = (s32[]{:T(128)}, f32[256,256]{1,0:T(8,128)}, s32[2,2]{1,0:T(2,128)S(1)}, f32[2,128,128]{2,1,0:T(8,128)S(1)}, s32[]{:T(128)}) while((s32[]{:T(128)}, f32[256,256]{1,0:T(8,128)}, s32[2,2]{1,0:T(2,128)S(1)}, f32[2,128,128]{2,1,0:T(8,128)S(1)}, s32[]{:T(128)}) %tuple.28), condition=%wide.while_cond, body=%wide.while_body.sunk | while | flops 2 | bytes 131189 | solution.py:13
  241.6 0.6 fusion.40
  242.2 2.3 bitcast_dynamic-update-slice_fusion.2
  244.6 0.6 fusion.40
  245.2 2.3 bitcast_dynamic-update-slice_fusion.2
  247.5 0.0 copy-start
  247.5 19.7 %custom-call.16 = f32[2,128,128]{1,2,0:T(8,128)S(1)} custom-call(f32[2,128,128]{2,1,0:T(8,128)S(1)} %get-tuple-element.10), custom_call_target="InvertDiagBlocksLowerTriangular" | custom-call | tf_op jit(solution)/shard_map/jit(_solve_triangular)/triangular_solve | solution.py:13
  267.2 0.6 fusion.34
  267.8 1.8 convolution_subtract_fusion
  269.7 0.0 copy-start.2
  269.7 0.6 convolution_convert_fusion
  270.3 0.9 fusion
  271.3 1.9 fusion.14
  273.2 0.0 all-reduce.9.cloned.1.call-update
  273.3 149.4 %all-reduce.9.cloned.1.call-done = f32[1024,256]{1,0:T(8,128)} async-done(((f32[1024,256]{1,0:T(8,128)}), f32[1024,256]{1,0:T(8,128)}) %all-reduce.9.cloned.1.call-update) | async-done | bytes 1048592 | tf_op jit(solution)/shard_map/psum | solution.py:34
  422.6 1.4 multiply_reduce_fusion
  424.0 17.3 %psum.31 = f32[256]{0:T(256)S(1)} all-reduce(f32[256]{0:T(256)S(1)} %multiply_reduce_fusion), channel_id=1, replica_groups=mesh['dp'=4,'fsdp'=8,'tensor'=8] {'tensor'}, use_global_device_ids=true, to_apply=%region_8.9 | all-reduce | flops 256 | bytes 2048 | tf_op jit(solution)/shard_map/psum | solution.py:35
  441.3 1.3 multiply_divide_fusion
  442.6 0.0 copy-start.6
  442.6 0.0 copy-start.3
  442.7 2.1 multiply_convert_fusion
  444.8 0.3 copy-done.3
  445.0 0.6 copy-done.4
  445.6 2.9 subtract_bitcast_fusion
  (16 shorter events, 0.1 us)
Async XLA Ops:
  7.2 2.8 copy-start.7
  7.2 2.9 copy-start.1
  7.2 123.8 %all-reduce.5.cloned.1.call-start = ((), (), s32[]{:S(2)}) async-start(), calls=%async_computation | async-start | bytes 2097152 | tf_op jit(solution)/shard_map/psum | solution.py:30
  11.7 191.2 %all-reduce.7.cloned.1.call-start = ((), (), s32[]{:S(2)}) async-start(), calls=%async_computation.1 | async-start | bytes 524288 | tf_op jit(solution)/shard_map/psum | solution.py:31
  131.0 4.4 copy-start.5
  135.2 287.4 %all-reduce.9.cloned.1.call-start = ((), (), s32[]{:S(2)}) async-start(), calls=%async_computation.2 | async-start | bytes 2097152 | tf_op jit(solution)/shard_map/psum | solution.py:34
  247.5 22.9 %copy-start = (bf16[1,1024,1024]{2,1,0:T(8,128)(2,1)S(1)}, bf16[1,1024,1024]{2,1,0:T(8,128)(2,1)}, u32[]{:S(2)}) copy-start(bf16[1,1024,1024]{2,1,0:T(8,128)(2,1)} %param.4) | copy-start | bytes 6291460
  269.7 1.6 copy-start.2
  442.6 6.0 %copy-start.6 = (f32[1024,256]{1,0:T(8,128)}, f32[1024,256]{1,0:T(8,128)S(1)}, u32[]{:S(2)}) copy-start(f32[1024,256]{1,0:T(8,128)S(1)} %multiply_divide_fusion) | copy-start | bytes 3145732
  442.6 2.4 copy-start.3
  442.7 3.0 copy-start.4
Sparse Core Ops, SparseCore 0:
  11.9 119.1 all-reduce.4
  135.3 67.5 all-reduce.6
  273.4 149.1 all-reduce.8
where the time goes:
time: 456 us; the launch traced here: 455 us
  waiting for transfers between devices  336 us (74%)
  other arithmetic  58.1 us (13%)
  matrix products  20.1 us (4%)
  blocking collectives  17.3 us (4%)
  between operations  15.3 us (3%)
  local copies, waits for them, and re-layouts  7.94 us (2%)
    psum x1, waiting for transfers between devices, local(): right = lax.psum(partial_right, ('dp', 'fsdp')) / replicas  149 us
    psum x1, waiting for transfers between devices, local(): left = lax.psum(partial_left, ('dp', 'tensor')) / replicas  119 us
    psum x1, waiting for transfers between devices, local(): gram = lax.psum(jnp.dot(left.T, left, precision=highest), 'fsdp')  67.4 us
    another operation x6, other arithmetic, orthonormal(): lower = jnp.linalg.cholesky(gram)  33.9 us
    another operation x3, other arithmetic, orthonormal(): return jax.scipy.linalg.solve_triangular(lower, rows_part.T, lower=True).T  20.4 us
    psum x1, blocking collectives, local(): square_sums = lax.psum(jnp.sum(right * right, axis=0), 'tensor')  17.3 us
  transfers between devices with their start and end apart: 3, of which 3 were waited for; matrix products, arithmetic and copies ran while one was open for 0% of the time, Pallas kernels for 0%

commit v1 on v0

--- a/solution.py
+++ b/solution.py
@@ -31,7 +31,10 @@
     gram = lax.psum(jnp.dot(left.T, left, precision=highest), "fsdp")
     ortho_low = orthonormal(left, gram).astype(jnp.bfloat16)
     partial_right = transposed_product(moment, ortho_low) + transposed_product(change, ortho_low)
-    right = lax.psum(partial_right, ("dp", "fsdp")) / replicas
+    see_the_stops_all = lambda original, axis_id, bus_axis: lax.psum(
+        lax.psum(original, axis_id), bus_axis
+    )
+    right = see_the_stops_all(partial_right, "fsdp", "dp") / replicas
     square_sums = lax.psum(jnp.sum(right * right, axis=0), "tensor")
     new_factor = right / jnp.sqrt(square_sums / COLS + 1e-06)
     right_low = right.astype(jnp.bfloat16)

time: 456 us -> 433 us (0.950)
  waiting for transfers between devices: 336 us -> 316 us
    psum x1 -> x2, waiting for transfers between devices: 149 us -> 130 us  [the longest x1 75.2 us: local(): lax.psum(original, axis_id)]
  transfers between devices with their start and end apart: 3 -> 4, of which waited for: 3 -> 4; matrix products, arithmetic and copies ran while one was open for 0% -> 0% of each run, Pallas kernels for 0% -> 0%
where the time goes in v1:
time: 433 us; the launch traced here: 432 us
  waiting for transfers between devices  316 us (73%)
  other arithmetic  58.1 us (13%)
  matrix products  20.1 us (5%)
  between operations  15.3 us (4%)
  blocking collectives  14.3 us (3%)
  local copies, waits for them, and re-layouts  7.94 us (2%)
    psum x1, waiting for transfers between devices, local(): left = lax.psum(partial_left, ('dp', 'tensor')) / replicas  119 us
    psum x1, waiting for transfers between devices, local(): lax.psum(original, axis_id)  75.2 us
    psum x1, waiting for transfers between devices, local(): gram = lax.psum(jnp.dot(left.T, left, precision=highest), 'fsdp')  67.4 us
    psum x1, waiting for transfers between devices, local(): lax.psum(lax.psum(original, axis_id), bus_axis)  54.4 us
    another operation x6, other arithmetic, orthonormal(): lower = jnp.linalg.cholesky(gram)  33.9 us
    another operation x3, other arithmetic, orthonormal(): return jax.scipy.linalg.solve_triangular(lower, rows_part.T, lower=True).T  20.4 us
    psum x1, blocking collectives, local(): square_sums = lax.psum(jnp.sum(right * right, axis=0), 'tensor')  14.3 us
  transfers between devices with their start and end apart: 4, of which 4 were waited for; matrix products, arithmetic and copies ran while one was open for 0% of the time, Pallas kernels for 0%

profile of v1, /device:TPU:1, one launch (start us, length us, event | category | flops | bytes accessed | tf_op | source)
XLA Modules:
  0.0 432.5 jit_solution(70751014315420243)
XLA Ops:
  7.2 0.0 copy-start.1
  7.2 0.0 all-reduce.6.cloned.1.call-start
  7.2 2.7 fusion.2
  10.0 0.1 copy-done.1
  10.0 1.7 fusion.8
  11.7 0.0 all-reduce.6.cloned.1.call-update
  11.7 0.0 all-reduce.8.cloned.1.call-start
  11.8 119.2 %all-reduce.6.cloned.1.call-done = f32[1024,256]{1,0:T(8,128)} async-done(((f32[1024,256]{1,0:T(8,128)}), f32[1024,256]{1,0:T(8,128)}) %all-reduce.6.cloned.1.call-update) | async-done | bytes 1048592 | tf_op jit(solution)/shard_map/psum | solution.py:30
  131.0 4.2 fusion.17
  135.2 0.0 all-reduce.8.cloned.1.call-update
  135.2 0.2 all-reduce.10.cloned.1.call-start
  135.5 0.1 multiply_bitcast_fusion
  135.5 67.4 %all-reduce.8.cloned.1.call-done = f32[256,256]{0,1:T(8,128)} async-done(((f32[256,256]{0,1:T(8,128)}), f32[256,256]{0,1:T(8,128)}) %all-reduce.8.cloned.1.call-update) | async-done | bytes 262160 | tf_op jit(solution)/shard_map/psum | solution.py:31
  203.0 1.1 copy.7
  204.1 1.0 fusion.24
  205.1 11.7 %cholesky.50 = f32[128,128]{1,0:T(8,128)S(1)} custom-call(f32[128,128]{1,0:T(8,128)S(1)} %cholesky.118), custom_call_target="Cholesky" | custom-call | tf_op jit(solution)/shard_map/jit(cholesky)/cholesky | solution.py:12
  216.8 9.8 %custom-call.15 = f32[1,128,128]{1,2,0:T(8,128)S(1)} custom-call(f32[1,128,128]{2,1,0:T(8,128)S(1)} %get-tuple-element.24), custom_call_target="InvertDiagBlocksLowerTriangular" | custom-call | tf_op jit(solution)/shard_map/jit(cholesky)/cholesky | solution.py:12
  226.7 0.2 constant_dynamic-update-slice_fusion.1
  226.9 0.3 convolution_subtract_fusion.1
  227.1 11.7 %cholesky.105 = f32[128,128]{1,0:T(8,128)S(1)} custom-call(f32[128,128]{1,0:T(8,128)S(1)} %convolution_subtract_fusion.1), custom_call_target="Cholesky" | custom-call | tf_op jit(solution)/shard_map/jit(cholesky)/cholesky | solution.py:12
  238.9 0.6 compare_reduce_fusion
  240.8 0.7 select_select_fusion
  241.6 0.1 triangular_solve.57
  241.6 5.8 %while.1 = (s32[]{:T(128)}, f32[256,256]{1,0:T(8,128)}, s32[2,2]{1,0:T(2,128)S(1)}, f32[2,128,128]{2,1,0:T(8,128)S(1)}, s32[]{:T(128)}) while((s32[]{:T(128)}, f32[256,256]{1,0:T(8,128)}, s32[2,2]{1,0:T(2,128)S(1)}, f32[2,128,128]{2,1,0:T(8,128)S(1)}, s32[]{:T(128)}) %tuple.28), condition=%wide.while_cond, body=%wide.while_body.sunk | while | flops 2 | bytes 131189 | solution.py:13
  241.6 0.6 fusion.40
  242.2 2.3 bitcast_dynamic-update-slice_fusion.2
  244.6 0.6 fusion.40
  245.2 2.3 bitcast_dynamic-update-slice_fusion.2
  247.5 0.0 copy-start
  247.5 19.7 %custom-call.16 = f32[2,128,128]{1,2,0:T(8,128)S(1)} custom-call(f32[2,128,128]{2,1,0:T(8,128)S(1)} %get-tuple-element.10), custom_call_target="InvertDiagBlocksLowerTriangular" | custom-call | tf_op jit(solution)/shard_map/jit(_solve_triangular)/triangular_solve | solution.py:13
  267.2 0.6 fusion.34
  267.8 1.8 convolution_subtract_fusion
  269.7 0.0 copy-start.2
  269.7 0.6 convolution_convert_fusion
  270.3 0.9 fusion
  271.3 1.9 fusion.14
  273.2 0.0 all-reduce.10.cloned.1.call-update
  273.3 0.0 all-reduce.12.cloned.1.call-start
  273.3 75.2 %all-reduce.10.cloned.1.call-done = f32[1024,256]{1,0:T(8,128)} async-done(((f32[1024,256]{1,0:T(8,128)}), f32[1024,256]{1,0:T(8,128)}) %all-reduce.10.cloned.1.call-update) | async-done | bytes 1048592 | tf_op jit(solution)/shard_map/psum | solution.py:35
  348.5 0.0 all-reduce.12.cloned.1.call-update
  348.6 54.4 %all-reduce.12.cloned.1.call-done = f32[1024,256]{1,0:T(8,128)} async-done(((f32[1024,256]{1,0:T(8,128)}), f32[1024,256]{1,0:T(8,128)}) %all-reduce.12.cloned.1.call-update) | async-done | bytes 1048592 | tf_op jit(solution)/shard_map/psum | solution.py:34
  403.0 1.4 multiply_reduce_fusion
  404.4 14.3 %psum.39 = f32[256]{0:T(256)S(1)} all-reduce(f32[256]{0:T(256)S(1)} %multiply_reduce_fusion), channel_id=1, replica_groups=mesh['dp'=4,'fsdp'=8,'tensor'=8] {'tensor'}, use_global_device_ids=true, to_apply=%region_9.10 | all-reduce | flops 256 | bytes 2048 | tf_op jit(solution)/shard_map/psum | solution.py:38
  418.7 1.3 multiply_divide_fusion
  420.0 2.1 multiply_convert_fusion
  422.1 0.3 copy-done.3
  422.4 0.6 copy-done.4
  423.0 2.9 subtract_bitcast_fusion
  (19 shorter events, 0.2 us)
Async XLA Ops:
  7.2 2.8 copy-start.7
  7.2 2.9 copy-start.1
  7.2 123.8 %all-reduce.6.cloned.1.call-start = ((), (), s32[]{:S(2)}) async-start(), calls=%async_computation | async-start | bytes 2097152 | tf_op jit(solution)/shard_map/psum | solution.py:30
  11.7 191.2 %all-reduce.8.cloned.1.call-start = ((), (), s32[]{:S(2)}) async-start(), calls=%async_computation.1 | async-start | bytes 524288 | tf_op jit(solution)/shard_map/psum | solution.py:31
  131.0 4.4 %copy-start.5 = (f32[1024,256]{1,0:T(8,128)S(1)}, f32[1024,256]{1,0:T(8,128)}, u32[]{:S(2)}) copy-start(f32[1024,256]{1,0:T(8,128)} %all-reduce.6.cloned.1.call-done) | copy-start | bytes 3145732
  135.2 213.3 %all-reduce.10.cloned.1.call-start = ((), (), s32[]{:S(2)}) async-start(), calls=%async_computation.2 | async-start | bytes 2097152 | tf_op jit(solution)/shard_map/psum | solution.py:35
  247.5 22.9 %copy-start = (bf16[1,1024,1024]{2,1,0:T(8,128)(2,1)S(1)}, bf16[1,1024,1024]{2,1,0:T(8,128)(2,1)}, u32[]{:S(2)}) copy-start(bf16[1,1024,1024]{2,1,0:T(8,128)(2,1)} %param.4) | copy-start | bytes 6291460
  269.7 1.6 copy-start.2
  273.3 129.7 %all-reduce.12.cloned.1.call-start = ((), (), s32[]{:S(2)}) async-start(), calls=%async_computation.3 | async-start | bytes 2097152 | tf_op jit(solution)/shard_map/psum | solution.py:34
  420.0 6.0 %copy-start.6 = (f32[1024,256]{1,0:T(8,128)}, f32[1024,256]{1,0:T(8,128)S(1)}, u32[]{:S(2)}) copy-start(f32[1024,256]{1,0:T(8,128)S(1)} %multiply_divide_fusion) | copy-start | bytes 3145732
  420.0 2.4 copy-start.3
  420.0 3.0 copy-start.4
Sparse Core Ops, SparseCore 0:
  11.9 119.1 all-reduce.5
  135.3 67.5 all-reduce.7
  273.4 75.1 all-reduce.9
  350.8 52.1 all-reduce.11
